TPU v7x, 32 devices: a whole 2x2x4 slice. The times are simulated.
32 devices in a mesh: grp: 4 (over z), ep: 8 (over y, x, core), tp: 1.
Axes of the slice: x: 2, y: 2, z: 4, core: 2. Of those that a mesh axis runs over, the one named last changes fastest.
Arguments:
- tokens: bfloat16 [4096, 2048], P(('grp', 'ep'), 'tp'), may hold values from -6 to 6
- expert_ids: int32 [4096, 4], P(('grp', 'ep')), may hold values from 0 to 31, all different within a row; in each aligned block of 128 rows (0 to 127, 128 to 255, ...) at most 24 rows name the same one
- router_probs: float32 [4096, 4], P(('grp', 'ep')), may hold values from 0.02 to 1
- cotangent: bfloat16 [4096, 2048], P(('grp', 'ep'), 'tp'), may hold values from -6 to 6
- w_gate: bfloat16 [32, 2048, 768], P(('grp', 'ep'), None, 'tp'), may hold values from -0.125 to 0.125
- w_up: bfloat16 [32, 2048, 768], P(('grp', 'ep'), None, 'tp'), may hold values from -0.125 to 0.125
- w_down: bfloat16 [32, 768, 2048], P(('grp', 'ep'), 'tp'), may hold values from -0.21875 to 0.21875
Outputs:
- layer_out: bfloat16 [4096, 2048], P(('grp', 'ep'), 'tp')
- grad_tokens: bfloat16 [4096, 2048], P(('grp', 'ep'), 'tp')
- grad_gate: bfloat16 [32, 2048, 768], P(('grp', 'ep'), None, 'tp')
- grad_up: bfloat16 [32, 2048, 768], P(('grp', 'ep'), None, 'tp')
- grad_down: bfloat16 [32, 768, 2048], P(('grp', 'ep'), 'tp')
Inputs may be any that keep to these rules, and one draw needn't show every extreme that they name: `expert_ids`: each token names 4 different experts. Among the 128 rows of one index of grp+ep no expert is named by more than 24 tokens, and in some such block one expert is named by exactly 24.
All inputs are finite; a program needn't handle non-finite values.
Results may differ from a plain program's by a relative error of at most 0.0085.
Values may be sent and summed in bfloat16 or wider, within the bound.
A program may use at most 128 MiB of HBM per device.

v0:
```python
import jax
import jax.numpy as jnp
from jax import lax
from jax.sharding import PartitionSpec as P


def move_rows(first_rows, second_rows):
    return (
        lax.all_to_all(first_rows, ("grp", "ep"), split_axis=0, concat_axis=0, tiled=True),
        lax.all_to_all(second_rows, ("grp", "ep"), split_axis=0, concat_axis=0, tiled=True),
    )


def expert_math(rows_full, grads_full, gate_local, up_local, down_local):
    contract_last = (((1,), (1,)), ((), ()))
    contract_first = (((0,), (0,)), ((), ()))
    gate_pre = jnp.dot(rows_full, gate_local, preferred_element_type=jnp.float32)
    up_pre = jnp.dot(rows_full, up_local, preferred_element_type=jnp.float32)
    sigmoid_gate = jax.nn.sigmoid(gate_pre)
    activated = gate_pre * sigmoid_gate
    hidden = (activated * up_pre).astype(jnp.bfloat16)
    out_partial = jnp.dot(hidden, down_local, preferred_element_type=jnp.float32)
    grad_hidden = lax.dot_general(
        grads_full, down_local, contract_last, preferred_element_type=jnp.float32
    )
    grad_gate_pre = (
        grad_hidden * up_pre * sigmoid_gate * (1.0 + gate_pre * (1.0 - sigmoid_gate))
    ).astype(jnp.bfloat16)
    grad_up_pre = (grad_hidden * activated).astype(jnp.bfloat16)
    input_partial = lax.dot_general(
        grad_gate_pre, gate_local, contract_last, preferred_element_type=jnp.float32
    ) + lax.dot_general(grad_up_pre, up_local, contract_last, preferred_element_type=jnp.float32)
    down_grad_t = lax.dot_general(
        grads_full, hidden, contract_first, preferred_element_type=jnp.float32
    )
    gate_grad = lax.dot_general(
        rows_full, grad_gate_pre, contract_first, preferred_element_type=jnp.float32
    )
    up_grad = lax.dot_general(
        rows_full, grad_up_pre, contract_first, preferred_element_type=jnp.float32
    )
    return (out_partial, input_partial, gate_grad, up_grad, down_grad_t)


def on_device(tokens, expert_ids, router_probs, cotangent, w_gate, w_up, w_down):
    groups = lax.axis_size("grp")
    experts = groups * lax.axis_size("ep")
    tok_rows = tokens.shape[0]
    top_count = expert_ids.shape[1]
    capacity = 3 * tok_rows * top_count // (2 * experts)
    slot_count = experts * capacity
    combine = router_probs / jnp.sum(router_probs, axis=1, keepdims=True)
    flat_ids = expert_ids.reshape(-1)
    onehot = (flat_ids[:, None] == jnp.arange(experts, dtype=jnp.int32)[None, :]).astype(jnp.int32)
    before = jnp.cumsum(onehot, axis=0) - onehot
    slot_rank = jnp.sum(before * onehot, axis=1)
    slot_of = flat_ids * capacity + slot_rank
    chosen = jnp.arange(slot_count, dtype=jnp.int32)[:, None] == slot_of[None, :]
    owner_token = jnp.arange(tok_rows * top_count, dtype=jnp.int32) // top_count
    slot_token = jnp.sum(jnp.where(chosen, owner_token[None, :], 0), axis=1)
    filled = jnp.any(chosen, axis=1)
    slot_weight = jnp.sum(jnp.where(chosen, combine.reshape(-1)[None, :], 0.0), axis=1)
    selector = jnp.logical_and(
        slot_token[:, None] == jnp.arange(tok_rows, dtype=jnp.int32)[None, :], filled[:, None]
    )
    select_bf = selector.astype(jnp.bfloat16)
    sent_rows = jnp.dot(select_bf, tokens, preferred_element_type=jnp.float32).astype(jnp.bfloat16)
    sent_grads = (
        slot_weight[:, None] * jnp.dot(select_bf, cotangent, preferred_element_type=jnp.float32)
    ).astype(jnp.bfloat16)
    arrived_rows, arrived_grads = move_rows(sent_rows, sent_grads)
    rows_full, grads_full = (
        lax.all_gather(arrived_rows, "tp", axis=1, tiled=True),
        lax.all_gather(arrived_grads, "tp", axis=1, tiled=True),
    )
    out_partial, input_partial, gate_grad, up_grad, down_grad_t = expert_math(
        rows_full, grads_full, w_gate[0], w_up[0], w_down[0]
    )
    out_half, input_half = (
        lax.psum_scatter(out_partial, "tp", scatter_dimension=1, tiled=True),
        lax.psum_scatter(input_partial, "tp", scatter_dimension=1, tiled=True),
    )
    back_local = out_half.astype(jnp.bfloat16)
    input_local = input_half.astype(jnp.bfloat16)
    grad_gate_local = gate_grad.astype(jnp.bfloat16)
    grad_up_local = up_grad.astype(jnp.bfloat16)
    grad_down_local = down_grad_t.T.astype(jnp.bfloat16)
    back_out, back_input = move_rows(back_local, input_local)
    contract_first = (((0,), (0,)), ((), ()))
    weighted = slot_weight[:, None] * back_out.astype(jnp.float32)
    weighted_high = weighted.astype(jnp.bfloat16)
    weighted_low = (weighted - weighted_high.astype(jnp.float32)).astype(jnp.bfloat16)
    layer_sum = lax.dot_general(
        select_bf, weighted_high, contract_first, preferred_element_type=jnp.float32
    ) + lax.dot_general(select_bf, weighted_low, contract_first, preferred_element_type=jnp.float32)
    layer_out = layer_sum.astype(jnp.bfloat16)
    grad_tokens = lax.dot_general(
        select_bf, back_input, contract_first, preferred_element_type=jnp.float32
    ).astype(jnp.bfloat16)
    return (
        layer_out,
        grad_tokens,
        grad_gate_local[None],
        grad_up_local[None],
        grad_down_local[None],
    )


def solution(mesh):
    return jax.shard_map(
        on_device,
        mesh=mesh,
        in_specs=(
            P(("grp", "ep"), "tp"),
            P(("grp", "ep"), None),
            P(("grp", "ep"), None),
            P(("grp", "ep"), "tp"),
            P(("grp", "ep"), None, "tp"),
            P(("grp", "ep"), None, "tp"),
            P(("grp", "ep"), "tp", None),
        ),
        out_specs=(
            P(("grp", "ep"), "tp"),
            P(("grp", "ep"), "tp"),
            P(("grp", "ep"), None, "tp"),
            P(("grp", "ep"), None, "tp"),
            P(("grp", "ep"), "tp", None),
        ),
        check_vma=False,
    )
```

profile of v0, /device:TPU:0, one launch (start us, length us, event | category | flops | bytes accessed | tf_op | source)
XLA Modules:
  0.0 335.0 jit_solution(1954494858404100053)
XLA Ops:
  0.6 0.0 copy-start
  0.6 0.9 copy.16
  1.6 0.1 eq.53
  1.7 0.1 reshape.66
  1.8 1.2 reduce-window.6
  3.0 0.2 slice_reduce_fusion
  3.2 0.1 fusion.40
  3.4 0.2 fusion.21
  3.6 0.2 select_reduce_fusion.1
  3.9 3.7 %convolution_convert_fusion.4 = bf16[768,2048]{1,0:T(8,128)(2,1)} fusion(bf16[128,2048]{1,0:T(8,128)(2,1)} %param.7, s32[768]{0:T(1024)S(1)} %select_reduce_fusion.1, pred[768]{0:T(1024)(128)(4,1)S(1)} %fusion.21), kind=kOutput, calls=%fused_computation.10 | convolution fusion | flops 404422656 | bytes 3673856 | tf_op jit(solution)/shard_map/dot_general | solution.py:67
  7.6 0.0 copy-start.1
  7.6 7.4 %all-to-all-start = ((bf16[32,24,2048]{2,1,0:T(8,128)(2,1)}), bf16[32,24,2048]{2,1,0:T(8,128)(2,1)}, u32[]{:S(2)}, u32[]{:S(2)}) async-start(bf16[32,24,2048]{2,1,0:T(8,128)(2,1)} %bitcast.69), calls=%async_computation | async-start | bytes 6291456 | tf_op jit(solution)/shard_map/all_to_all | solution.py:9
  15.0 0.0 copy-done.1
  15.1 0.1 copy.19
  15.2 0.1 broadcast_in_dim.47
  15.3 0.2 select_reduce_fusion
  15.6 3.8 %multiply_convert_fusion = bf16[768,2048]{1,0:T(8,128)(2,1)} fusion(bf16[128,2048]{1,0:T(8,128)(2,1)} %param.10, f32[768]{0:T(1024)S(1)} %select_reduce_fusion, s32[768]{0:T(1024)S(1)} %select_reduce_fusion.1, pred[768]{0:T(1024)(128)(4,1)S(1)} %fusion.21), kind=kOutput, calls=%fused_computation.5 | convolution fusion | flops 405995520 | bytes 3676928 | tf_op jit(solution)/shard_map/dot_general | solution.py:69
  19.3 67.0 %all-to-all-done = bf16[32,24,2048]{2,1,0:T(8,128)(2,1)} async-done(((bf16[32,24,2048]{2,1,0:T(8,128)(2,1)}), bf16[32,24,2048]{2,1,0:T(8,128)(2,1)}, u32[]{:S(2)}, u32[]{:S(2)}) %all-to-all-start) | async-done | bytes 3145760 | tf_op jit(solution)/shard_map/all_to_all | solution.py:9
  86.4 4.3 %all-to-all-start.2 = ((bf16[32,24,2048]{2,1,0:T(8,128)(2,1)}), bf16[32,24,2048]{2,1,0:T(8,128)(2,1)}, u32[]{:S(2)}, u32[]{:S(2)}) async-start(bf16[32,24,2048]{2,1,0:T(8,128)(2,1)} %bitcast.68), calls=%async_computation.2 | async-start | bytes 6291456 | tf_op jit(solution)/shard_map/all_to_all | solution.py:10
  90.7 0.0 copy-start.3
  90.7 7.0 %fusion.13 = f32[768,768]{1,0:T(8,128)} fusion(bf16[768,2048]{1,0:T(8,128)(2,1)} %bitcast.2, bf16[1,2048,768]{2,1,0:T(8,128)(2,1)} %param.11), kind=kOutput, calls=%fused_computation.20 | convolution fusion | flops 2415919104 | bytes 8650752 | tf_op jit(solution)/shard_map/dot_general | solution.py:17
  97.7 0.0 copy-done.3
  97.7 5.9 %fusion.9 = f32[768,768]{1,0:T(8,128)} fusion(bf16[768,2048]{1,0:T(8,128)(2,1)} %bitcast.2, bf16[1,2048,768]{2,1,0:T(8,128)(2,1)S(1)} %copy-done.3), kind=kOutput, calls=%fused_computation.16 | convolution fusion | flops 2415919104 | bytes 8650752 | tf_op jit(solution)/shard_map/dot_general | solution.py:18
  103.6 58.3 %all-to-all-done.2 = bf16[32,24,2048]{2,1,0:T(8,128)(2,1)} async-done(((bf16[32,24,2048]{2,1,0:T(8,128)(2,1)}), bf16[32,24,2048]{2,1,0:T(8,128)(2,1)}, u32[]{:S(2)}, u32[]{:S(2)}) %all-to-all-start.2) | async-done | bytes 3145760 | tf_op jit(solution)/shard_map/all_to_all | solution.py:10
  162.0 0.0 copy-done
  162.0 0.0 copy-start.2
  162.0 7.8 %multiply_convert_fusion.1 = (bf16[768,768]{1,0:T(8,128)(2,1)S(1)}, bf16[768,768]{1,0:T(8,128)(2,1)S(1)}, bf16[768,768]{1,0:T(8,128)(2,1)}) fusion(f32[768,768]{1,0:T(8,128)} %fusion.13, f32[768,768]{1,0:T(8,128)} %fusion.9, bf16[768,2048]{1,0:T(8,128)(2,1)} %bitcast.9, bf16[1,768,2048]{2,1,0:T(8,128)(2,1)S(1)} %copy-done), kind=kOutput, calls=%fused_computation.29 | convolution fusion | flops 2424766464 | bytes 14548992 | tf_op jit(solution)/shard_map/dot_general | solution.py:23
  169.8 0.0 copy-done.2
  169.8 2.6 fusion.11
  172.4 0.0 copy-done.5
  172.4 0.0 copy-done.7
  172.5 0.1 copy-done.4
  172.5 4.0 %add_convert_fusion = bf16[768,2048]{1,0:T(8,128)(2,1)} fusion(f32[768,2048]{1,0:T(8,128)S(1)} %fusion.11, bf16[768,768]{1,0:T(8,128)(2,1)S(1)} %get-tuple-element.5, bf16[1,2048,768]{2,1,0:T(8,128)(2,1)S(1)} %copy-done.4), kind=kOutput, calls=%fused_computation.4 | convolution fusion | flops 2419064832 | bytes 13762560 | tf_op jit(solution)/shard_map/dot_general | solution.py:32
  176.5 4.0 %all-to-all-start.3 = ((bf16[32,24,2048]{2,1,0:T(8,128)(2,1)}), bf16[32,24,2048]{2,1,0:T(8,128)(2,1)}, u32[]{:S(2)}, u32[]{:S(2)}) async-start(bf16[32,24,2048]{2,1,0:T(8,128)(2,1)} %bitcast.71), calls=%async_computation.3 | async-start | bytes 6291456 | tf_op jit(solution)/shard_map/all_to_all | solution.py:10
  180.6 5.3 %convolution_convert_fusion.3 = bf16[768,2048]{1,0:T(8,128)(2,1)} fusion(bf16[768,768]{1,0:T(8,128)(2,1)} %get-tuple-element.7, bf16[1,768,2048]{2,1,0:T(8,128)(2,1)S(1)} %copy-done), kind=kOutput, calls=%fused_computation.9 | convolution fusion | flops 2417491968 | bytes 7471104 | tf_op jit(solution)/shard_map/dot_general | solution.py:22
  185.8 66.1 %all-to-all-done.3 = bf16[32,24,2048]{2,1,0:T(8,128)(2,1)} async-done(((bf16[32,24,2048]{2,1,0:T(8,128)(2,1)}), bf16[32,24,2048]{2,1,0:T(8,128)(2,1)}, u32[]{:S(2)}, u32[]{:S(2)}) %all-to-all-start.3) | async-done | bytes 3145760 | tf_op jit(solution)/shard_map/all_to_all | solution.py:10
  251.9 4.4 %all-to-all-start.1 = ((bf16[32,24,2048]{2,1,0:T(8,128)(2,1)}), bf16[32,24,2048]{2,1,0:T(8,128)(2,1)}, u32[]{:S(2)}, u32[]{:S(2)}) async-start(bf16[32,24,2048]{2,1,0:T(8,128)(2,1)} %bitcast.70), calls=%async_computation.1 | async-start | bytes 6291456 | tf_op jit(solution)/shard_map/all_to_all | solution.py:9
  256.3 0.0 copy-start.6
  256.3 6.7 %fusion.18 = bf16[1,768,2048]{2,1,0:T(8,128)(2,1)} fusion(bf16[768,768]{1,0:T(8,128)(2,1)} %get-tuple-element.7, bf16[768,2048]{1,0:T(8,128)(2,1)} %bitcast.9), kind=kOutput, calls=%fused_computation.25 | convolution fusion | flops 2417491968 | bytes 7471104 | tf_op jit(solution)/shard_map/dot_general | solution.py:33
  262.9 0.0 copy-done.6
  262.9 6.3 %fusion.16 = bf16[1,2048,768]{2,1,0:T(8,128)(2,1)} fusion(bf16[768,2048]{1,0:T(8,128)(2,1)} %bitcast.2, bf16[768,768]{1,0:T(8,128)(2,1)S(1)} %copy-done.6), kind=kOutput, calls=%fused_computation.23 | convolution fusion | flops 2417491968 | bytes 7471104 | tf_op jit(solution)/shard_map/dot_general | solution.py:36
  269.3 0.0 copy-done.8
  269.3 6.2 %fusion.17 = bf16[1,2048,768]{2,1,0:T(8,128)(2,1)} fusion(bf16[768,2048]{1,0:T(8,128)(2,1)} %bitcast.2, bf16[768,768]{1,0:T(8,128)(2,1)S(1)} %copy-done.8), kind=kOutput, calls=%fused_computation.24 | convolution fusion | flops 2417491968 | bytes 7471104 | tf_op jit(solution)/shard_map/dot_general | solution.py:39
  275.5 3.5 %convolution_convert_fusion.5 = bf16[128,2048]{1,0:T(8,128)(2,1)} fusion(bf16[768,2048]{1,0:T(8,128)(2,1)} %bitcast.11, s32[768]{0:T(1024)S(1)} %select_reduce_fusion.1, pred[768]{0:T(1024)(128)(4,1)S(1)} %fusion.21), kind=kOutput, calls=%fused_computation.28 | convolution fusion | flops 403111936 | bytes 3673856 | tf_op jit(solution)/shard_map/dot_general | solution.py:97
  279.0 48.5 %all-to-all-done.1 = bf16[32,24,2048]{2,1,0:T(8,128)(2,1)} async-done(((bf16[32,24,2048]{2,1,0:T(8,128)(2,1)}), bf16[32,24,2048]{2,1,0:T(8,128)(2,1)}, u32[]{:S(2)}, u32[]{:S(2)}) %all-to-all-start.1) | async-done | bytes 3145760 | tf_op jit(solution)/shard_map/all_to_all | solution.py:9
  327.5 2.5 fusion.1
  330.0 3.4 %fusion.3 = f32[128,2048]{1,0:T(8,128)S(1)} fusion(bf16[768,2048]{1,0:T(8,128)(2,1)} %bitcast.15, bf16[768,2048]{1,0:T(8,128)(2,1)S(1)} %fusion.1, f32[768]{0:T(1024)S(1)} %select_reduce_fusion, s32[768]{0:T(1024)S(1)} %select_reduce_fusion.1, pred[768]{0:T(1024)(128)(4,1)S(1)} %fusion.21), kind=kOutput, calls=%fused_computation.11 | convolution fusion | flops 410714112 | bytes 7346944 | tf_op jit(solution)/shard_map/dot_general | solution.py:95
  333.4 1.6 fusion.19
  (10 shorter events, 0.1 us)
Async XLA Ops:
  0.6 161.3 %copy-start = (bf16[1,768,2048]{2,1,0:T(8,128)(2,1)S(1)}, bf16[1,768,2048]{2,1,0:T(8,128)(2,1)}, u32[]{:S(2)}) copy-start(bf16[1,768,2048]{2,1,0:T(8,128)(2,1)} %param.13) | copy-start | bytes 9437188
  7.6 7.5 %copy-start.1 = (f32[128,4]{0,1:T(4,128)S(1)}, f32[128,4]{0,1:T(4,128)}, u32[]{:S(2)}) copy-start(f32[128,4]{0,1:T(4,128)} %param.9) | copy-start | bytes 6148
  7.6 78.8 %all-to-all-start = ((bf16[32,24,2048]{2,1,0:T(8,128)(2,1)}), bf16[32,24,2048]{2,1,0:T(8,128)(2,1)}, u32[]{:S(2)}, u32[]{:S(2)}) async-start(bf16[32,24,2048]{2,1,0:T(8,128)(2,1)} %bitcast.69), calls=%async_computation | async-start | bytes 6291456 | tf_op jit(solution)/shard_map/all_to_all | solution.py:9
  86.4 75.6 %all-to-all-start.2 = ((bf16[32,24,2048]{2,1,0:T(8,128)(2,1)}), bf16[32,24,2048]{2,1,0:T(8,128)(2,1)}, u32[]{:S(2)}, u32[]{:S(2)}) async-start(bf16[32,24,2048]{2,1,0:T(8,128)(2,1)} %bitcast.68), calls=%async_computation.2 | async-start | bytes 6291456 | tf_op jit(solution)/shard_map/all_to_all | solution.py:10
  90.7 7.0 %copy-start.3 = (bf16[1,2048,768]{2,1,0:T(8,128)(2,1)S(1)}, bf16[1,2048,768]{2,1,0:T(8,128)(2,1)}, u32[]{:S(2)}) copy-start(bf16[1,2048,768]{2,1,0:T(8,128)(2,1)} %param.12) | copy-start | bytes 9437188
  162.0 7.8 %copy-start.2 = (bf16[1,2048,768]{2,1,0:T(8,128)(2,1)S(1)}, bf16[1,2048,768]{2,1,0:T(8,128)(2,1)}, u32[]{:S(2)}) copy-start(bf16[1,2048,768]{2,1,0:T(8,128)(2,1)} %param.11) | copy-start | bytes 9437188
  169.8 2.7 copy-start.5
  169.8 2.7 copy-start.7
  169.8 2.7 copy-start.4
  176.5 75.4 %all-to-all-start.3 = ((bf16[32,24,2048]{2,1,0:T(8,128)(2,1)}), bf16[32,24,2048]{2,1,0:T(8,128)(2,1)}, u32[]{:S(2)}, u32[]{:S(2)}) async-start(bf16[32,24,2048]{2,1,0:T(8,128)(2,1)} %bitcast.71), calls=%async_computation.3 | async-start | bytes 6291456 | tf_op jit(solution)/shard_map/all_to_all | solution.py:10
  251.9 75.6 %all-to-all-start.1 = ((bf16[32,24,2048]{2,1,0:T(8,128)(2,1)}), bf16[32,24,2048]{2,1,0:T(8,128)(2,1)}, u32[]{:S(2)}, u32[]{:S(2)}) async-start(bf16[32,24,2048]{2,1,0:T(8,128)(2,1)} %bitcast.70), calls=%async_computation.1 | async-start | bytes 6291456 | tf_op jit(solution)/shard_map/all_to_all | solution.py:9
  256.3 6.7 %copy-start.6 = (bf16[768,768]{1,0:T(8,128)(2,1)S(1)}, bf16[768,768]{1,0:T(8,128)(2,1)}, u32[]{:S(2)}) copy-start(bf16[768,768]{1,0:T(8,128)(2,1)} %copy-done.5) | copy-start | bytes 3538948
  262.9 6.3 %copy-start.8 = (bf16[768,768]{1,0:T(8,128)(2,1)S(1)}, bf16[768,768]{1,0:T(8,128)(2,1)}, u32[]{:S(2)}) copy-start(bf16[768,768]{1,0:T(8,128)(2,1)} %copy-done.7) | copy-start | bytes 3538948
where the time goes:
time: 336 us; the launch traced here: 335 us
  waiting for transfers between devices  240 us (71%)
  matrix products  67.8 us (20%)
  starting transfers between devices  20.2 us (6%)
  other arithmetic  4.53 us (1%)
    all_to_all x2, waiting for transfers between devices, move_rows(): lax.all_to_all(second_rows, ('grp', 'ep'), split_axis=0, concat_axis=0, t...  124 us
    all_to_all x2, waiting for transfers between devices, move_rows(): lax.all_to_all(first_rows, ('grp', 'ep'), split_axis=0, concat_axis=0, ti...  116 us
    all_to_all x2, starting transfers between devices, move_rows(): lax.all_to_all(first_rows, ('grp', 'ep'), split_axis=0, concat_axis=0, ti...  11.8 us
    all_to_all x2, starting transfers between devices, move_rows(): lax.all_to_all(second_rows, ('grp', 'ep'), split_axis=0, concat_axis=0, t...  8.35 us
    dot_general x1, matrix products, expert_math(): lax.dot_general(grads_full, down_local, contract_last, preferred_element_...  7.83 us
    dot_general x1, matrix products, expert_math(): jnp.dot(rows_full, gate_local, preferred_element_type=jnp.float32)  6.99 us
  transfers between devices with their start and end apart: 4, of which 4 were waited for; matrix products, arithmetic and copies ran while one was open for 13% of the time, Pallas kernels for 0%

commit v1 on v0

v1 whole, which is shorter than its diff:
```python
import jax
import jax.numpy as jnp
from jax import lax
from jax.sharding import PartitionSpec as P

F32 = jnp.float32
BF16 = jnp.bfloat16


def expert_math(rows_full, grads_full, gate_local, up_local, down_local):
    contract_last = (((1,), (1,)), ((), ()))
    contract_first = (((0,), (0,)), ((), ()))
    gate_pre = jnp.dot(rows_full, gate_local, preferred_element_type=F32)
    up_pre = jnp.dot(rows_full, up_local, preferred_element_type=F32)
    sigmoid_gate = jax.nn.sigmoid(gate_pre)
    activated = gate_pre * sigmoid_gate
    hidden = (activated * up_pre).astype(BF16)
    out_partial = jnp.dot(hidden, down_local, preferred_element_type=F32)
    grad_hidden = lax.dot_general(grads_full, down_local, contract_last, preferred_element_type=F32)
    grad_gate_pre = (
        grad_hidden * up_pre * sigmoid_gate * (1.0 + gate_pre * (1.0 - sigmoid_gate))
    ).astype(BF16)
    grad_up_pre = (grad_hidden * activated).astype(BF16)
    input_partial = lax.dot_general(
        grad_gate_pre, gate_local, contract_last, preferred_element_type=F32
    ) + lax.dot_general(grad_up_pre, up_local, contract_last, preferred_element_type=F32)
    down_grad = lax.dot_general(hidden, grads_full, contract_first, preferred_element_type=F32)
    gate_grad = lax.dot_general(rows_full, grad_gate_pre, contract_first, preferred_element_type=F32)
    up_grad = lax.dot_general(rows_full, grad_up_pre, contract_first, preferred_element_type=F32)
    return (out_partial, input_partial, gate_grad, up_grad, down_grad)


def on_device(tokens, expert_ids, router_probs, cotangent, w_gate, w_up, w_down):
    groups = lax.axis_size("grp")
    plane = lax.axis_size("ep")
    experts = groups * plane
    tok_rows, width = tokens.shape
    top_count = expert_ids.shape[1]
    capacity = 3 * tok_rows * top_count // (2 * experts)
    combine = router_probs / jnp.sum(router_probs, axis=1, keepdims=True)
    packed = jnp.concatenate([expert_ids.astype(F32), combine], axis=1)
    packed_all = lax.all_gather(packed, "grp", axis=0, tiled=False)
    tokens_all = lax.all_gather(tokens, "grp", axis=0, tiled=False)
    cot_all = lax.all_gather(cotangent, "grp", axis=0, tiled=False)
    ids_all = packed_all[:, :, :top_count]
    weight_all = packed_all[:, :, top_count:]
    mine = lax.axis_index("grp") * plane + jnp.arange(plane, dtype=jnp.int32)
    hits = ids_all[None] == mine.astype(F32)[:, None, None, None]
    member = jnp.any(hits, axis=3)
    weight = jnp.sum(jnp.where(hits, weight_all[None], 0.0), axis=3)
    count = member.astype(jnp.int32)
    rank = jnp.cumsum(count, axis=2) - count
    slots = jnp.arange(capacity, dtype=jnp.int32)
    chosen = jnp.logical_and(
        rank[:, :, None, :] == slots[None, None, :, None], member[:, :, None, :]
    )
    select_bf = chosen.astype(BF16)
    weighted = jnp.where(chosen, weight[:, :, None, :], 0.0)
    slot_weight = jnp.sum(weighted, axis=3)
    weight_bf = weighted.astype(BF16)

    def spread(blocks):
        return jnp.einsum("ezst,ztd->ezsd", select_bf, blocks, preferred_element_type=F32)

    def swap(rows):
        return lax.all_to_all(rows, "ep", split_axis=0, concat_axis=0, tiled=True)

    sent_rows = spread(tokens_all).astype(BF16)
    sent_grads = (slot_weight[..., None] * spread(cot_all)).astype(BF16)
    flat = (experts * capacity, width)
    rows_full = lax.all_gather(swap(sent_rows).reshape(flat), "tp", axis=1, tiled=True)
    grads_full = lax.all_gather(swap(sent_grads).reshape(flat), "tp", axis=1, tiled=True)
    out_partial, input_partial, gate_grad, up_grad, down_grad = expert_math(
        rows_full, grads_full, w_gate[0], w_up[0], w_down[0]
    )
    out_half = lax.psum_scatter(out_partial, "tp", scatter_dimension=1, tiled=True)
    input_half = lax.psum_scatter(input_partial, "tp", scatter_dimension=1, tiled=True)
    shape = (plane, groups, capacity, width)

    def gather_back(rows, select):
        back = swap(rows.astype(BF16).reshape(shape))
        part = jnp.einsum("ezst,ezsd->ztd", select, back, preferred_element_type=F32)
        part = part.astype(BF16).reshape(groups * tok_rows, width)
        return lax.psum_scatter(part, "grp", scatter_dimension=0, tiled=True)

    layer_out = gather_back(out_half, weight_bf)
    grad_tokens = gather_back(input_half, select_bf)
    return (
        layer_out.astype(BF16),
        grad_tokens.astype(BF16),
        gate_grad.astype(BF16)[None],
        up_grad.astype(BF16)[None],
        down_grad.astype(BF16)[None],
    )


def solution(mesh):
    return jax.shard_map(
        on_device,
        mesh=mesh,
        in_specs=(
            P(("grp", "ep"), "tp"),
            P(("grp", "ep"), None),
            P(("grp", "ep"), None),
            P(("grp", "ep"), "tp"),
            P(("grp", "ep"), None, "tp"),
            P(("grp", "ep"), None, "tp"),
            P(("grp", "ep"), "tp", None),
        ),
        out_specs=(
            P(("grp", "ep"), "tp"),
            P(("grp", "ep"), "tp"),
            P(("grp", "ep"), None, "tp"),
            P(("grp", "ep"), None, "tp"),
            P(("grp", "ep"), "tp", None),
        ),
        check_vma=False,
    )
```

time: 336 us -> 302 us (0.90)
  waiting for transfers between devices: 240 us -> 115 us
  blocking collectives: 0 us -> 95.5 us
  between operations: 0.79 us -> 13.9 us
  starting transfers between devices: 20.2 us -> 9.25 us
  matrix products: 67.8 us -> 58.9 us
    all_to_all x4 -> x2, waiting for transfers between devices: 240 us -> 24.7 us  [swap(): return lax.all_to_all(rows, 'ep', split_axis=0, concat_axis=0, tiled=True)]
    all_to_all x0 -> x2, blocking collectives: none -> 80.5 us  [swap(): return lax.all_to_all(rows, 'ep', split_axis=0, concat_axis=0, tiled=True)]
    all_gather x0 -> x2, waiting for transfers between devices: none -> 67.7 us  [the longest x1 36.7 us: on_device(): cot_all = lax.all_gather(cotangent, 'grp', axis=0, tiled=False)]
    reduce_scatter x0 -> x2, waiting for transfers between devices: none -> 21.7 us  [gather_back(): return lax.psum_scatter(part, 'grp', scatter_dimension=0, tiled=True)]
    all_gather x0 -> x1, blocking collectives: none -> 15 us  [on_device(): packed_all = lax.all_gather(packed, 'grp', axis=0, tiled=False)]
    all_to_all x4 -> x2, starting transfers between devices: 20.2 us -> 8.91 us  [swap(): return lax.all_to_all(rows, 'ep', split_axis=0, concat_axis=0, tiled=True)]
    dot_general x9 -> x8, matrix products: 40.8 us -> 33 us  [the longest x1 6.99 us: expert_math(): up_pre = jnp.dot(rows_full, up_local, preferred_element_type=F32)]
    convert_element_type x0 -> x2, local copies, waits for them, and re-layouts: none -> 4.16 us  [the longest x1 2.08 us: on_device(): sent_rows = spread(tokens_all).astype(BF16)]
  transfers between devices with their start and end apart: 4 -> 6, of which waited for: 4 -> 4; matrix products, arithmetic and copies ran while one was open for 13% -> 17% of each run, Pallas kernels for 0% -> 0%
where the time goes in v1:
time: 302 us; the launch traced here: 301 us
  waiting for transfers between devices  115 us (38%)
  blocking collectives  95.5 us (32%)
  matrix products  58.9 us (20%)
  between operations  13.9 us (5%)
  starting transfers between devices  9.25 us (3%)
  local copies, waits for them, and re-layouts  4.28 us (1%)
  other arithmetic  3.59 us (1%)
    all_to_all x2, blocking collectives, swap(): return lax.all_to_all(rows, 'ep', split_axis=0, concat_axis=0, tiled=True)  80.5 us
    all_gather x1, waiting for transfers between devices, on_device(): cot_all = lax.all_gather(cotangent, 'grp', axis=0, tiled=False)  36.7 us
    all_gather x1, waiting for transfers between devices, on_device(): tokens_all = lax.all_gather(tokens, 'grp', axis=0, tiled=False)  31 us
    all_to_all x2, waiting for transfers between devices, swap(): return lax.all_to_all(rows, 'ep', split_axis=0, concat_axis=0, tiled=True)  24.7 us
    reduce_scatter x2, waiting for transfers between devices, gather_back(): return lax.psum_scatter(part, 'grp', scatter_dimension=0, tiled=True)  21.7 us
    all_gather x1, blocking collectives, on_device(): packed_all = lax.all_gather(packed, 'grp', axis=0, tiled=False)  15 us
    all_to_all x2, starting transfers between devices, swap(): return lax.all_to_all(rows, 'ep', split_axis=0, concat_axis=0, tiled=True)  8.91 us
    dot_general x1, matrix products, expert_math(): lax.dot_general(grads_full, down_local, contract_last, preferred_element_...  7.83 us
  transfers between devices with their start and end apart: 6, of which 4 were waited for; matrix products, arithmetic and copies ran while one was open for 17% of the time, Pallas kernels for 0%

profile of v1, /device:TPU:0, one launch (start us, length us, event | category | flops | bytes accessed | tf_op | source)
XLA Modules:
  0.0 300.9 jit_solution(442465078978447529)
XLA Ops:
  7.2 0.0 copy-start
  7.2 0.0 all-gather.6.cloned.1.call-start
  7.2 0.7 all-gather.6.cloned.1.call-update
  7.9 0.0 all-gather.8.cloned.1.call-start
  8.0 0.7 all-gather.8.cloned.1.call-update
  8.7 0.7 reduce_sum.27
  9.4 0.7 broadcast_divide_fusion
  10.1 0.7 convert_element_type.64
  10.8 15.0 %all-gather = f32[512,8]{0,1:T(8,128)S(1)} all-gather(f32[128,8]{0,1:T(8,128)S(1)} %pad_maximum_fusion), channel_id=2, replica_groups=mesh['grp'=4,'ep'=8,'tp'=1] {'grp'}, dimensions={0}, use_global_device_ids=true | all-gather | bytes 20480 | tf_op jit(solution)/shard_map/all_gather | solution.py:42
  25.7 0.1 compare_reduce_fusion
  25.8 1.1 reduce_window_sum.11
  27.0 31.0 %all-gather.6.cloned.1.call-done = bf16[512,2048]{1,0:T(8,128)(2,1)} async-done(((bf16[128,2048]{1,0:T(8,128)(2,1)}), bf16[512,2048]{1,0:T(8,128)(2,1)}) %all-gather.6.cloned.1.call-update) | async-done | bytes 2097168 | tf_op jit(solution)/shard_map/all_gather | solution.py:43
  58.0 2.6 fusion.13
  60.6 2.1 copy.28
  62.7 4.5 %all-to-all-start = ((bf16[8,4,24,2048]{3,2,1,0:T(8,128)(2,1)}), bf16[8,4,24,2048]{3,2,1,0:T(8,128)(2,1)}, u32[]{:S(2)}, u32[]{:S(2)}) async-start(bf16[8,4,24,2048]{3,2,1,0:T(8,128)(2,1)} %copy.28), calls=%async_computation | async-start | bytes 6291456 | tf_op jit(solution)/shard_map/all_to_all | solution.py:66
  67.1 0.1 fusion.32
  67.2 0.2 select_reduce_fusion
  67.4 36.7 %all-gather.8.cloned.1.call-done = bf16[512,2048]{1,0:T(8,128)(2,1)} async-done(((bf16[128,2048]{1,0:T(8,128)(2,1)}), bf16[512,2048]{1,0:T(8,128)(2,1)}) %all-gather.8.cloned.1.call-update) | async-done | bytes 2097168 | tf_op jit(solution)/shard_map/all_gather | solution.py:44
  104.1 2.6 fusion
  106.6 2.1 copy.30
  108.7 0.0 all-to-all-done
  108.7 4.4 %all-to-all-start.2 = ((bf16[8,4,24,2048]{3,2,1,0:T(8,128)(2,1)}), bf16[8,4,24,2048]{3,2,1,0:T(8,128)(2,1)}, u32[]{:S(2)}, u32[]{:S(2)}) async-start(bf16[8,4,24,2048]{3,2,1,0:T(8,128)(2,1)} %copy.30), calls=%async_computation.3 | async-start | bytes 6291456 | tf_op jit(solution)/shard_map/all_to_all | solution.py:66
  113.2 0.2 reduce-scatter.5.cloned.1.call-start
  113.4 0.0 copy-start.1
  113.4 7.0 %fusion.5 = f32[768,768]{1,0:T(8,128)} fusion(bf16[768,2048]{1,0:T(8,128)(2,1)} %bitcast.5, bf16[1,2048,768]{2,1,0:T(8,128)(2,1)} %param.12), kind=kOutput, calls=%fused_computation.14 | convolution fusion | flops 2415919104 | bytes 8650752 | tf_op jit(solution)/shard_map/dot_general | solution.py:14
  120.4 0.0 copy-done.1
  120.4 5.9 %fusion.9 = f32[768,768]{1,0:T(8,128)} fusion(bf16[768,2048]{1,0:T(8,128)(2,1)} %bitcast.5, bf16[1,2048,768]{2,1,0:T(8,128)(2,1)S(1)} %copy-done.1), kind=kOutput, calls=%fused_computation.18 | convolution fusion | flops 2415919104 | bytes 8650752 | tf_op jit(solution)/shard_map/dot_general | solution.py:13
  126.3 24.7 %all-to-all-done.2 = bf16[8,4,24,2048]{3,2,1,0:T(8,128)(2,1)} async-done(((bf16[8,4,24,2048]{3,2,1,0:T(8,128)(2,1)}), bf16[8,4,24,2048]{3,2,1,0:T(8,128)(2,1)}, u32[]{:S(2)}, u32[]{:S(2)}) %all-to-all-start.2) | async-done | bytes 3145760 | tf_op jit(solution)/shard_map/all_to_all | solution.py:66
  151.0 0.0 copy-done
  151.0 7.8 %multiply_convert_fusion = (bf16[768,768]{1,0:T(8,128)(2,1)S(1)}, bf16[768,768]{1,0:T(8,128)(2,1)S(1)}, bf16[768,768]{1,0:T(8,128)(2,1)}) fusion(f32[768,768]{1,0:T(8,128)} %fusion.9, f32[768,768]{1,0:T(8,128)} %fusion.5, bf16[768,2048]{1,0:T(8,128)(2,1)} %bitcast.17, bf16[1,768,2048]{2,1,0:T(8,128)(2,1)S(1)} %copy-done), kind=kOutput, calls=%fused_computation.26 | convolution fusion | flops 2424766464 | bytes 14548992 | tf_op jit(solution)/shard_map/dot_general | solution.py:19
  158.9 0.0 copy-done.2
  158.9 2.6 fusion.7
  161.5 0.0 copy-done.4
  161.5 0.1 copy-done.3
  161.6 2.9 add_convert_fusion
  164.5 40.3 %all_to_all.20 = bf16[8,4,24,2048]{3,2,1,0:T(8,128)(2,1)S(1)} all-to-all(bf16[8,4,24,2048]{3,2,1,0:T(8,128)(2,1)S(1)} %bitcast.70), channel_id=1, replica_groups=mesh['grp'=4,'ep'=8,'tp'=1] {'ep'}, dimensions={0} | all-to-all | bytes 6291456 | tf_op jit(solution)/shard_map/all_to_all | solution.py:66
  204.7 2.1 bitcast_convert_fusion
  206.9 0.0 reduce-scatter.5.cloned.1.call-update
  206.9 0.0 reduce-scatter.3.cloned.1.call-start
  206.9 4.1 %convolution_convert_fusion.3 = bf16[768,2048]{1,0:T(8,128)(2,1)S(1)} fusion(bf16[768,768]{1,0:T(8,128)(2,1)} %get-tuple-element.7, bf16[1,768,2048]{2,1,0:T(8,128)(2,1)S(1)} %copy-done), kind=kOutput, calls=%fused_computation.8 | convolution fusion | flops 2417491968 | bytes 7471104 | tf_op jit(solution)/shard_map/dot_general | solution.py:18
  211.0 40.3 %all_to_all.21 = bf16[8,4,24,2048]{3,2,1,0:T(8,128)(2,1)S(1)} all-to-all(bf16[8,4,24,2048]{3,2,1,0:T(8,128)(2,1)S(1)} %bitcast.71), channel_id=1, replica_groups=mesh['grp'=4,'ep'=8,'tp'=1] {'ep'}, dimensions={0} | all-to-all | bytes 6291456 | tf_op jit(solution)/shard_map/all_to_all | solution.py:66
  251.3 2.1 bitcast_convert_fusion.1
  253.4 0.0 reduce-scatter.3.cloned.1.call-update
  253.5 0.0 copy-start.5
  253.5 6.7 %fusion.16 = bf16[1,768,2048]{2,1,0:T(8,128)(2,1)} fusion(bf16[768,768]{1,0:T(8,128)(2,1)} %get-tuple-element.7, bf16[768,2048]{1,0:T(8,128)(2,1)} %bitcast.17), kind=kOutput, calls=%fused_computation.25 | convolution fusion | flops 2417491968 | bytes 7471104 | tf_op jit(solution)/shard_map/dot_general | solution.py:27
  260.1 6.3 %fusion.14 = bf16[1,2048,768]{2,1,0:T(8,128)(2,1)} fusion(bf16[768,2048]{1,0:T(8,128)(2,1)} %bitcast.5, bf16[768,768]{1,0:T(8,128)(2,1)S(1)} %copy-done.5), kind=kOutput, calls=%fused_computation.23 | convolution fusion | flops 2417491968 | bytes 7471104 | tf_op jit(solution)/shard_map/dot_general | solution.py:28
  266.5 6.2 %fusion.15 = bf16[1,2048,768]{2,1,0:T(8,128)(2,1)} fusion(bf16[768,2048]{1,0:T(8,128)(2,1)} %bitcast.5, bf16[768,768]{1,0:T(8,128)(2,1)S(1)} %copy-done.7), kind=kOutput, calls=%fused_computation.24 | convolution fusion | flops 2417491968 | bytes 7471104 | tf_op jit(solution)/shard_map/dot_general | solution.py:29
  272.7 21.7 %reduce-scatter.3.cloned.1.call-done = bf16[128,2048]{1,0:T(8,128)(2,1)} async-done(((bf16[512,2048]{1,0:T(8,128)(2,1)}), bf16[128,2048]{1,0:T(8,128)(2,1)}) %reduce-scatter.3.cloned.1.call-update) | async-done | bytes 524304 | tf_op jit(solution)/shard_map/reduce_scatter | solution.py:84
  (14 shorter events, 0.0 us)
Async XLA Ops:
  7.2 143.9 %copy-start = (bf16[1,768,2048]{2,1,0:T(8,128)(2,1)S(1)}, bf16[1,768,2048]{2,1,0:T(8,128)(2,1)}, u32[]{:S(2)}) copy-start(bf16[1,768,2048]{2,1,0:T(8,128)(2,1)} %param.13) | copy-start | bytes 9437188
  7.2 50.8 %all-gather.6.cloned.1.call-start = ((), (), s32[]{:S(2)}) async-start(), calls=%async_computation.8 | async-start | bytes 2621440 | tf_op jit(solution)/shard_map/all_gather | solution.py:43
  7.9 96.2 %all-gather.8.cloned.1.call-start = ((), (), s32[]{:S(2)}) async-start(), calls=%async_computation.9 | async-start | bytes 2621440 | tf_op jit(solution)/shard_map/all_gather | solution.py:44
  62.7 46.1 %all-to-all-start = ((bf16[8,4,24,2048]{3,2,1,0:T(8,128)(2,1)}), bf16[8,4,24,2048]{3,2,1,0:T(8,128)(2,1)}, u32[]{:S(2)}, u32[]{:S(2)}) async-start(bf16[8,4,24,2048]{3,2,1,0:T(8,128)(2,1)} %copy.28), calls=%async_computation | async-start | bytes 6291456 | tf_op jit(solution)/shard_map/all_to_all | solution.py:66
  108.7 42.3 %all-to-all-start.2 = ((bf16[8,4,24,2048]{3,2,1,0:T(8,128)(2,1)}), bf16[8,4,24,2048]{3,2,1,0:T(8,128)(2,1)}, u32[]{:S(2)}, u32[]{:S(2)}) async-start(bf16[8,4,24,2048]{3,2,1,0:T(8,128)(2,1)} %copy.30), calls=%async_computation.3 | async-start | bytes 6291456 | tf_op jit(solution)/shard_map/all_to_all | solution.py:66
  113.2 159.5 %reduce-scatter.5.cloned.1.call-start = ((), (), s32[]{:S(2)}) async-start(), calls=%async_computation.7 | async-start | bytes 2621440 | tf_op jit(solution)/shard_map/reduce_scatter | solution.py:84
  113.4 7.0 %copy-start.1 = (bf16[1,2048,768]{2,1,0:T(8,128)(2,1)S(1)}, bf16[1,2048,768]{2,1,0:T(8,128)(2,1)}, u32[]{:S(2)}) copy-start(bf16[1,2048,768]{2,1,0:T(8,128)(2,1)} %param.11) | copy-start | bytes 9437188
  151.0 7.8 %copy-start.2 = (bf16[1,2048,768]{2,1,0:T(8,128)(2,1)S(1)}, bf16[1,2048,768]{2,1,0:T(8,128)(2,1)}, u32[]{:S(2)}) copy-start(bf16[1,2048,768]{2,1,0:T(8,128)(2,1)} %param.11) | copy-start | bytes 9437188
  158.9 2.6 copy-start.4
  158.9 2.7 copy-start.6
  158.9 2.7 copy-start.3
  206.9 87.5 %reduce-scatter.3.cloned.1.call-start = ((), (), s32[]{:S(2)}) async-start(), calls=%async_computation.6 | async-start | bytes 2621440 | tf_op jit(solution)/shard_map/reduce_scatter | solution.py:84
  253.5 6.7 %copy-start.5 = (bf16[768,768]{1,0:T(8,128)(2,1)S(1)}, bf16[768,768]{1,0:T(8,128)(2,1)}, u32[]{:S(2)}) copy-start(bf16[768,768]{1,0:T(8,128)(2,1)} %copy-done.4) | copy-start | bytes 3538948
  260.1 6.3 %copy-start.7 = (bf16[768,768]{1,0:T(8,128)(2,1)S(1)}, bf16[768,768]{1,0:T(8,128)(2,1)}, u32[]{:S(2)}) copy-start(bf16[768,768]{1,0:T(8,128)(2,1)} %copy-done.6) | copy-start | bytes 3538948
Sparse Core Ops, SparseCore 0:
  9.6 48.4 all-gather.5
  59.6 44.4 all-gather.7
  207.0 40.7 reduce-scatter.4
  253.6 40.7 reduce-scatter.2

commit v2 on v1

v2 whole, which is shorter than its diff:
```python
import functools

import jax
import jax.numpy as jnp
from jax import lax
from jax.experimental import pallas as pl
from jax.experimental.pallas import tpu as pltpu
from jax.sharding import PartitionSpec as P

F32 = jnp.float32
BF16 = jnp.bfloat16
MESH = pl.DeviceIdType.MESH


def expert_math(rows_full, grads_full, gate_local, up_local, down_local):
    contract_last = (((1,), (1,)), ((), ()))
    contract_first = (((0,), (0,)), ((), ()))
    gate_pre = jnp.dot(rows_full, gate_local, preferred_element_type=F32)
    up_pre = jnp.dot(rows_full, up_local, preferred_element_type=F32)
    sigmoid_gate = jax.nn.sigmoid(gate_pre)
    activated = gate_pre * sigmoid_gate
    hidden = (activated * up_pre).astype(BF16)
    out_partial = jnp.dot(hidden, down_local, preferred_element_type=F32)
    grad_hidden = lax.dot_general(grads_full, down_local, contract_last, preferred_element_type=F32)
    grad_gate_pre = (
        grad_hidden * up_pre * sigmoid_gate * (1.0 + gate_pre * (1.0 - sigmoid_gate))
    ).astype(BF16)
    grad_up_pre = (grad_hidden * activated).astype(BF16)
    input_partial = lax.dot_general(
        grad_gate_pre, gate_local, contract_last, preferred_element_type=F32
    ) + lax.dot_general(grad_up_pre, up_local, contract_last, preferred_element_type=F32)
    down_grad = lax.dot_general(hidden, grads_full, contract_first, preferred_element_type=F32)
    gate_grad = lax.dot_general(rows_full, grad_gate_pre, contract_first, preferred_element_type=F32)
    up_grad = lax.dot_general(rows_full, grad_up_pre, contract_first, preferred_element_type=F32)
    return (out_partial, input_partial, gate_grad, up_grad, down_grad)


def block_at(g, groups, i):
    low, high = g, groups - 1 - g
    near = jnp.minimum(low, high)
    inside = i <= 2 * near
    far = i - near
    half = (i + 1) // 2
    odd = lax.rem(i, 2)
    side_in = 1 - 2 * odd
    side_out = jnp.where(low < high, 1, -1)
    return g + jnp.where(inside, side_in * half, side_out * far)


def greet(groups, plane):
    g, me = lax.axis_index("grp"), lax.axis_index("ep")
    barrier = pltpu.get_barrier_semaphore()

    def signal_peer(j, carry):
        pl.semaphore_signal(
            barrier, inc=1, device_id={"ep": lax.rem(me + j, plane)}, device_id_type=MESH
        )
        return carry

    lax.fori_loop(1, plane, signal_peer, 0)

    @pl.when(g > 0)
    def _():
        pl.semaphore_signal(barrier, inc=1, device_id={"grp": g - 1}, device_id_type=MESH)

    @pl.when(g < groups - 1)
    def _():
        pl.semaphore_signal(barrier, inc=1, device_id={"grp": g + 1}, device_id_type=MESH)

    beside = jnp.minimum(g, 1) + jnp.minimum(groups - 1 - g, 1)
    pl.semaphore_wait(barrier, plane - 1 + beside)


def remote(src, dst, send, recv, device):
    return pltpu.make_async_remote_copy(
        src_ref=src, dst_ref=dst, send_sem=send, recv_sem=recv,
        device_id=device, device_id_type=MESH,
    )


def dispatch_kernel(
    groups, plane, capacity, top,
    meta_ref, tok_ref, cot_ref,
    rows_ref, grads_ref, select_ref, weight_ref,
    meta, blocks, stage, slot_w,
    own_sem, meta_send, meta_recv, up_send, down_send, z_recv, row_send, row_recv, self_sem,
):
    g, me = lax.axis_index("grp"), lax.axis_index("ep")
    tok_rows, width = tok_ref.shape
    chunk = min(width, 512)
    arrived = (rows_ref, grads_ref)
    own = [
        pltpu.make_async_copy(meta_ref, meta.at[g], own_sem.at[2]),
        pltpu.make_async_copy(tok_ref, blocks.at[0, g], own_sem.at[0]),
        pltpu.make_async_copy(cot_ref, blocks.at[1, g], own_sem.at[1]),
    ]
    for copy in own:
        copy.start()
    greet(groups, plane)
    for copy in own:
        copy.wait()

    def up_meta(s):
        return remote(meta.at[s], meta.at[s], meta_send.at[0, s], meta_recv.at[s], {"grp": g + 1})

    def down_meta(s):
        return remote(meta.at[s], meta.at[s], meta_send.at[1, s], meta_recv.at[s], {"grp": g - 1})

    def up_block(a, s):
        block = blocks.at[a, s]
        return remote(block, block, up_send.at[a, s], z_recv.at[a, s], {"grp": g + 1})

    def down_block(a, s):
        block = blocks.at[a, s]
        return remote(block, block, down_send.at[a, s], z_recv.at[a, s], {"grp": g - 1})

    def row_copy(a, s, j):
        e = lax.rem(me + j, plane)
        return remote(
            stage.at[a, s, e], arrived[a].at[me, s], row_send.at[a, s, j],
            row_recv.at[a, me, s], {"ep": e},
        )

    def self_copy(a, s):
        return pltpu.make_async_copy(
            stage.at[a, s, me], arrived[a].at[me, s], self_sem.at[a, s]
        )

    def goes_up(s):
        return jnp.logical_and(s <= g, g < groups - 1)

    def goes_down(s):
        return jnp.logical_and(s >= g, g > 0)

    def select_rows(s):
        info = meta[s]
        expert = g * plane + lax.broadcasted_iota(jnp.int32, (plane, tok_rows), 0)
        expert = expert.astype(F32)
        member = jnp.zeros((plane, tok_rows), F32)
        weight = jnp.zeros((plane, tok_rows), F32)
        for k in range(top):
            hit = info[k:k + 1, :] == expert
            member = jnp.where(hit, 1.0, member)
            weight = jnp.where(hit, info[top + k:top + k + 1, :], weight)
        earlier = lax.broadcasted_iota(jnp.int32, (tok_rows, tok_rows), 0)
        later = lax.broadcasted_iota(jnp.int32, (tok_rows, tok_rows), 1)
        before = jnp.where(earlier < later, 1.0, 0.0).astype(BF16)
        rank = jnp.dot(member.astype(BF16), before, preferred_element_type=F32)
        place = jnp.where(member > 0.0, rank, -1.0)
        slots = lax.broadcasted_iota(jnp.int32, (capacity, tok_rows), 0).astype(F32)
        picked, scaled = [], []
        for e in range(plane):
            chosen = place[e:e + 1, :] == slots
            picked.append(jnp.where(chosen, 1.0, 0.0))
            scaled.append(jnp.where(chosen, weight[e:e + 1, :], 0.0))
        picked, scaled = jnp.concatenate(picked, axis=0), jnp.concatenate(scaled, axis=0)
        select_ref[s] = picked.astype(BF16)
        weight_ref[s] = scaled.astype(BF16)
        slot_w[s] = jnp.sum(scaled, axis=1, keepdims=True)

    for a in range(2):

        def step(i, carry, a=a):
            s = block_at(g, groups, i)
            if a == 0:
                @pl.when(i > 0)
                def _():
                    down_meta(s).wait_recv()

                @pl.when(goes_up(s))
                def _():
                    up_meta(s).start()

                @pl.when(goes_down(s))
                def _():
                    down_meta(s).start()

            @pl.when(i > 0)
            def _():
                down_block(a, s).wait_recv()

            @pl.when(goes_up(s))
            def _():
                up_block(a, s).start()

            @pl.when(goes_down(s))
            def _():
                down_block(a, s).start()

            if a == 0:
                select_rows(s)
            for at in range(0, width, chunk):
                part = jnp.dot(
                    select_ref[s], blocks[a, s, :, at:at + chunk], preferred_element_type=F32
                )
                if a == 1:
                    part = part * slot_w[s]
                for e in range(plane):
                    stage[a, s, e, :, at:at + chunk] = part[
                        e * capacity:(e + 1) * capacity, :
                    ].astype(BF16)

            def send(j, inner):
                row_copy(a, s, j).start()
                return inner

            lax.fori_loop(1, plane, send, 0)
            self_copy(a, s).start()
            return carry

        lax.fori_loop(0, groups, step, 0)

    for a in range(2):

        def drain(s, carry, a=a):
            if a == 0:
                @pl.when(goes_up(s))
                def _():
                    up_meta(s).wait_send()

                @pl.when(goes_down(s))
                def _():
                    down_meta(s).wait_send()

            @pl.when(goes_up(s))
            def _():
                up_block(a, s).wait_send()

            @pl.when(goes_down(s))
            def _():
                down_block(a, s).wait_send()

            self_copy(a, s).wait()

            def finish(j, inner):
                e = lax.rem(me + j, plane)
                row_copy(a, s, j).wait_send()
                remote(
                    stage.at[a, s, e], arrived[a].at[e, s], row_send.at[a, s, j],
                    row_recv.at[a, e, s], {"ep": e},
                ).wait_recv()
                return inner

            lax.fori_loop(1, plane, finish, 0)
            return carry

        lax.fori_loop(0, groups, drain, 0)


def dispatch(groups, plane, capacity, top, meta, tokens, cotangent):
    tok_rows, width = tokens.shape
    slots = plane * capacity
    arrived = jax.ShapeDtypeStruct((plane, groups, capacity, width), BF16)
    chosen = jax.ShapeDtypeStruct((groups, slots, tok_rows), BF16)
    dma = pltpu.SemaphoreType.DMA
    return pl.pallas_call(
        functools.partial(dispatch_kernel, groups, plane, capacity, top),
        out_shape=(arrived, arrived, chosen, chosen),
        in_specs=[pl.BlockSpec(memory_space=pl.ANY)] * 3,
        out_specs=(pl.BlockSpec(memory_space=pl.ANY),) * 2
        + (pl.BlockSpec(memory_space=pltpu.VMEM),) * 2,
        scratch_shapes=[
            pltpu.VMEM((groups,) + meta.shape, F32),
            pltpu.VMEM((2, groups, tok_rows, width), BF16),
            pltpu.VMEM((2, groups, plane, capacity, width), BF16),
            pltpu.VMEM((groups, slots, 1), F32),
            dma((3,)), dma((2, groups)), dma((groups,)),
            dma((2, groups)), dma((2, groups)), dma((2, groups)),
            dma((2, groups, plane)), dma((2, plane, groups)), dma((2, groups)),
        ],
        compiler_params=pltpu.CompilerParams(
            collective_id=0, has_side_effects=True, vmem_limit_bytes=60 * 1024 * 1024
        ),
    )(meta, tokens, cotangent)


def combine_kernel(
    groups, plane, capacity,
    out_ref, inp_ref, select_ref, weight_ref,
    layer_ref, grad_ref,
    back, partial, from_low, from_high,
    row_send, row_recv, self_sem, up_send, down_send, low_recv, high_recv,
):
    g, me = lax.axis_index("grp"), lax.axis_index("ep")
    tok_rows, width = layer_ref.shape
    chunk = min(width, 512)
    sources, results, selects = (out_ref, inp_ref), (layer_ref, grad_ref), (weight_ref, select_ref)

    def row_copy(a, d, j):
        e = lax.rem(me + j, plane)
        return remote(
            sources[a].at[e, d], back.at[a, d, me], row_send.at[a, d, j],
            row_recv.at[a, me, d], {"ep": e},
        )

    def self_copy(a, d):
        return pltpu.make_async_copy(
            sources[a].at[me, d], back.at[a, d, me], self_sem.at[a, d]
        )

    def up_copy(a, d):
        return remote(
            partial.at[a, d], from_low.at[a, d], up_send.at[a, d], low_recv.at[a, d],
            {"grp": g + 1},
        )

    def down_copy(a, d):
        return remote(
            partial.at[a, d], from_high.at[a, d], down_send.at[a, d], high_recv.at[a, d],
            {"grp": g - 1},
        )

    greet(groups, plane)
    for a in range(2):

        def launch(i, carry, a=a):
            d = block_at(g, groups, groups - 1 - i)

            def send(j, inner):
                row_copy(a, d, j).start()
                return inner

            lax.fori_loop(1, plane, send, 0)
            self_copy(a, d).start()
            return carry

        lax.fori_loop(0, groups, launch, 0)

    for a in range(2):

        def step(i, carry, a=a):
            d = block_at(g, groups, groups - 1 - i)
            self_copy(a, d).wait()

            def arrive(j, inner):
                e = lax.rem(me + j, plane)
                row_copy(a, d, j).wait_send()
                remote(
                    sources[a].at[e, d], back.at[a, d, e], row_send.at[a, d, j],
                    row_recv.at[a, e, d], {"ep": e},
                ).wait_recv()
                return inner

            lax.fori_loop(1, plane, arrive, 0)
            has_low = jnp.logical_and(d >= g, g > 0)
            has_high = jnp.logical_and(d <= g, g < groups - 1)

            @pl.when(has_low)
            def _():
                up_copy(a, d).wait_recv()

            @pl.when(has_high)
            def _():
                down_copy(a, d).wait_recv()

            @pl.when(jnp.logical_not(has_low))
            def _():
                from_low[a, d] = jnp.zeros((tok_rows, width), BF16)

            @pl.when(jnp.logical_not(has_high))
            def _():
                from_high[a, d] = jnp.zeros((tok_rows, width), BF16)

            for at in range(0, width, chunk):
                cols = slice(at, at + chunk)
                rows = jnp.concatenate(
                    [back[a, d, e, :, cols].astype(F32) for e in range(plane)], axis=0
                ).astype(BF16)
                part = lax.dot_general(
                    selects[a][d], rows, (((0,), (0,)), ((), ())), preferred_element_type=F32
                )
                part = part + from_low[a, d, :, cols].astype(F32)
                part = part + from_high[a, d, :, cols].astype(F32)
                partial[a, d, :, cols] = part.astype(BF16)

            @pl.when(d > g)
            def _():
                up_copy(a, d).start()

            @pl.when(d < g)
            def _():
                down_copy(a, d).start()

            return carry

        lax.fori_loop(0, groups, step, 0)
        results[a][...] = partial[a, g]

    for a in range(2):

        def drain(d, carry, a=a):
            @pl.when(d > g)
            def _():
                up_copy(a, d).wait_send()

            @pl.when(d < g)
            def _():
                down_copy(a, d).wait_send()

            return carry

        lax.fori_loop(0, groups, drain, 0)


def gather_back(groups, plane, capacity, out_rows, in_rows, select, weight):
    tok_rows, width = select.shape[2], out_rows.shape[3]
    result = jax.ShapeDtypeStruct((tok_rows, width), BF16)
    dma = pltpu.SemaphoreType.DMA
    blocks = pltpu.VMEM((2, groups, tok_rows, width), BF16)
    return pl.pallas_call(
        functools.partial(combine_kernel, groups, plane, capacity),
        out_shape=(result, result),
        in_specs=[pl.BlockSpec(memory_space=pl.ANY)] * 2
        + [pl.BlockSpec(memory_space=pltpu.VMEM)] * 2,
        out_specs=(pl.BlockSpec(memory_space=pltpu.VMEM),) * 2,
        scratch_shapes=[
            pltpu.VMEM((2, groups, plane, capacity, width), BF16),
            blocks, blocks, blocks,
            dma((2, groups, plane)), dma((2, plane, groups)), dma((2, groups)),
            dma((2, groups)), dma((2, groups)), dma((2, groups)), dma((2, groups)),
        ],
        compiler_params=pltpu.CompilerParams(
            collective_id=1, has_side_effects=True, vmem_limit_bytes=60 * 1024 * 1024
        ),
    )(out_rows, in_rows, select, weight)


def on_device(tokens, expert_ids, router_probs, cotangent, w_gate, w_up, w_down):
    groups = lax.axis_size("grp")
    plane = lax.axis_size("ep")
    experts = groups * plane
    tok_rows, width = tokens.shape
    top = expert_ids.shape[1]
    capacity = -(-3 * tok_rows * top // (2 * experts) // 8) * 8
    combine = router_probs / jnp.sum(router_probs, axis=1, keepdims=True)
    meta = jnp.concatenate([expert_ids.astype(F32), combine], axis=1).T
    rows, grads, select, weight = dispatch(
        groups, plane, capacity, top, meta, tokens, cotangent
    )
    flat = (experts * capacity, width)
    rows_full = lax.all_gather(rows.reshape(flat), "tp", axis=1, tiled=True)
    grads_full = lax.all_gather(grads.reshape(flat), "tp", axis=1, tiled=True)
    out_partial, input_partial, gate_grad, up_grad, down_grad = expert_math(
        rows_full, grads_full, w_gate[0], w_up[0], w_down[0]
    )
    out_half = lax.psum_scatter(out_partial, "tp", scatter_dimension=1, tiled=True)
    input_half = lax.psum_scatter(input_partial, "tp", scatter_dimension=1, tiled=True)
    shape = (plane, groups, capacity, width)
    layer_out, grad_tokens = gather_back(
        groups, plane, capacity,
        out_half.astype(BF16).reshape(shape), input_half.astype(BF16).reshape(shape),
        select, weight,
    )
    return (
        layer_out,
        grad_tokens,
        gate_grad.astype(BF16)[None],
        up_grad.astype(BF16)[None],
        down_grad.astype(BF16)[None],
    )


def solution(mesh):
    return jax.shard_map(
        on_device,
        mesh=mesh,
        in_specs=(
            P(("grp", "ep"), "tp"),
            P(("grp", "ep"), None),
            P(("grp", "ep"), None),
            P(("grp", "ep"), "tp"),
            P(("grp", "ep"), None, "tp"),
            P(("grp", "ep"), None, "tp"),
            P(("grp", "ep"), "tp", None),
        ),
        out_specs=(
            P(("grp", "ep"), "tp"),
            P(("grp", "ep"), "tp"),
            P(("grp", "ep"), None, "tp"),
            P(("grp", "ep"), None, "tp"),
            P(("grp", "ep"), "tp", None),
        ),
        check_vma=False,
    )
```

time: 302 us -> 227 us (0.75)
  Pallas kernels: 0 us -> 184 us
  waiting for transfers between devices: 115 us -> 0 us
  blocking collectives: 95.5 us -> 0 us
  matrix products: 58.9 us -> 37 us
  between operations: 13.9 us -> 0.82 us
  starting transfers between devices: 9.25 us -> 0 us
    pallas_call x0 -> x2, Pallas kernels: none -> 184 us  [the longest x1 96.3 us: gather_back(): pl.pallas_call(functools.partial(combine_kernel, groups, plane, capacity)...]
    all_to_all x2 -> x0, blocking collectives: 80.5 us -> none  [swap(): return lax.all_to_all(rows, 'ep', split_axis=0, concat_axis=0, tiled=True)]
    all_gather x2 -> x0, waiting for transfers between devices: 67.7 us -> none  [the longest x1 36.7 us: on_device(): cot_all = lax.all_gather(cotangent, 'grp', axis=0, tiled=False)]
    all_to_all x2 -> x0, waiting for transfers between devices: 24.7 us -> none  [swap(): return lax.all_to_all(rows, 'ep', split_axis=0, concat_axis=0, tiled=True)]
    reduce_scatter x2 -> x0, waiting for transfers between devices: 21.7 us -> none  [gather_back(): return lax.psum_scatter(part, 'grp', scatter_dimension=0, tiled=True)]
    all_gather x1 -> x0, blocking collectives: 15 us -> none  [on_device(): packed_all = lax.all_gather(packed, 'grp', axis=0, tiled=False)]
    dot_general x4 -> x0, matrix products: 9.36 us -> none  [the longest x2 5.12 us: spread(): jnp.einsum('ezst,ztd->ezsd', select_bf, blocks, preferred_element_type=F32)]
    all_to_all x2 -> x0, starting transfers between devices: 8.91 us -> none  [swap(): return lax.all_to_all(rows, 'ep', split_axis=0, concat_axis=0, tiled=True)]
  transfers between devices with their start and end apart: 6 -> 0, of which waited for: 4 -> 0; matrix products, arithmetic and copies ran while one was open for 17% -> 0% of each run, Pallas kernels for 0% -> 0%
where the time goes in v2:
time: 227 us
  Pallas kernels  184 us (81%)
  matrix products  37 us (16%)
  other arithmetic  2.93 us (1%)
    pallas_call x1, Pallas kernels, gather_back(): pl.pallas_call(functools.partial(combine_kernel, groups, plane, capacity)...  96.3 us
    pallas_call x1, Pallas kernels, dispatch(): pl.pallas_call(functools.partial(dispatch_kernel, groups, plane, capacity...  87.7 us
    dot_general x1, matrix products, expert_math(): lax.dot_general(rows_full, grad_gate_pre, contract_first, preferred_eleme...  6.71 us
    dot_general x1, matrix products, expert_math(): up_pre = jnp.dot(rows_full, up_local, preferred_element_type=F32)  5.58 us

profile of v2, /device:TPU:0, one launch (start us, length us, event | category | flops | bytes accessed | tf_op | source)
XLA Modules:
  0.0 226.9 jit_solution(5337648919305673571)
XLA Ops:
  0.6 0.0 copy-start
  0.6 0.9 reduce_sum.9
  1.5 0.8 broadcast_divide_fusion
  2.3 0.7 convert_element_type.27
  3.0 0.6 maximum_bitcast_fusion.meta_ref
  3.6 87.7 %shard_map.110 = (bf16[8,4,24,2048]{3,2,1,0:T(8,128)(2,1)}, bf16[8,4,24,2048]{3,2,1,0:T(8,128)(2,1)}, bf16[4,192,128]{2,1,0:T(8,128)(2,1)}, bf16[4,192,128]{2,1,0:T(8,128)(2,1)}) custom-call(f32[8,128]{1,0:T(8,128)} %maximum_bitcast_fusion.meta_ref, bf16[128,2048]{1,0:T(8,128)(2,1)} %tok_ref.1, bf16[128,2048]{1,0:T(8,128)(2,1)} %cot_ref.1), custom_call_target="tpu_custom_call" | custom-call | tf_op jit(solution)/shard_map/pallas_call | solution.py:256
  91.3 0.0 copy-start.3
  91.3 0.0 copy-start.7
  91.3 5.6 %fusion.4 = f32[768,768]{1,0:T(8,128)S(1)} fusion(bf16[768,2048]{1,0:T(8,128)(2,1)} %bitcast.45, bf16[1,2048,768]{2,1,0:T(8,128)(2,1)} %param.12), kind=kOutput, calls=%fused_computation.9 | convolution fusion | flops 2415919104 | bytes 8650752 | tf_op jit(solution)/shard_map/dot_general | solution.py:19
  96.9 0.0 copy-done.3
  96.9 0.0 copy-done.7
  96.9 0.0 copy-start.5
  96.9 2.6 %fusion.8 = f32[768,768]{1,0:T(8,128)S(1)} fusion(bf16[768,2048]{1,0:T(8,128)(2,1)S(1)} %bitcast.47, bf16[1,2048,768]{2,1,0:T(8,128)(2,1)S(1)} %copy-done.3), kind=kOutput, calls=%fused_computation.13 | convolution fusion | flops 2415919104 | bytes 8650752 | tf_op jit(solution)/shard_map/dot_general | solution.py:18
  99.5 0.0 copy-done
  99.5 0.0 copy-done.5
  99.6 3.4 %multiply_convert_fusion = (bf16[768,768]{1,0:T(8,128)(2,1)S(1)}, bf16[768,768]{1,0:T(8,128)(2,1)S(1)}, bf16[768,768]{1,0:T(8,128)(2,1)S(1)}) fusion(f32[768,768]{1,0:T(8,128)S(1)} %fusion.8, f32[768,768]{1,0:T(8,128)S(1)} %fusion.4, bf16[768,2048]{1,0:T(8,128)(2,1)S(1)} %bitcast.43, bf16[1,768,2048]{2,1,0:T(8,128)(2,1)S(1)} %copy-done), kind=kOutput, calls=%fused_computation.18 | convolution fusion | flops 2424766464 | bytes 14548992 | tf_op jit(solution)/shard_map/dot_general | solution.py:24
  103.0 0.0 copy-start.9
  103.0 0.0 copy-start.12
  103.0 0.0 copy-start.10
  103.0 0.0 copy-start.4
  103.0 2.6 %fusion.6 = f32[768,2048]{1,0:T(8,128)S(1)} fusion(bf16[768,768]{1,0:T(8,128)(2,1)S(1)} %get-tuple-element.18, bf16[1,2048,768]{2,1,0:T(8,128)(2,1)S(1)} %copy-done.3), kind=kOutput, calls=%fused_computation.11 | convolution fusion | flops 2415919104 | bytes 10616832 | tf_op jit(solution)/shard_map/dot_general | solution.py:29
  105.7 0.0 copy-done.9
  105.7 0.0 copy-done.12
  105.7 0.5 copy-done.4
  106.2 4.0 %add_convert_fusion = bf16[768,2048]{1,0:T(8,128)(2,1)} fusion(f32[768,2048]{1,0:T(8,128)S(1)} %fusion.6, bf16[768,768]{1,0:T(8,128)(2,1)S(1)} %get-tuple-element.17, bf16[1,2048,768]{2,1,0:T(8,128)(2,1)S(1)} %copy-done.4), kind=kOutput, calls=%fused_computation | convolution fusion | flops 2419064832 | bytes 13762560 | tf_op jit(solution)/shard_map/dot_general | solution.py:31
  110.2 0.0 copy-done.10
  110.2 4.0 %convolution_convert_fusion.3 = bf16[768,2048]{1,0:T(8,128)(2,1)} fusion(bf16[768,768]{1,0:T(8,128)(2,1)S(1)} %get-tuple-element.19, bf16[1,768,2048]{2,1,0:T(8,128)(2,1)S(1)} %copy-done), kind=kOutput, calls=%fused_computation.4 | convolution fusion | flops 2417491968 | bytes 7471104 | tf_op jit(solution)/shard_map/dot_general | solution.py:23
  114.1 96.3 %shard_map.111 = (bf16[128,2048]{1,0:T(8,128)(2,1)}, bf16[128,2048]{1,0:T(8,128)(2,1)}) custom-call(bf16[8,4,24,2048]{3,2,1,0:T(8,128)(2,1)} %bitcast.42, bf16[8,4,24,2048]{3,2,1,0:T(8,128)(2,1)} %bitcast.41, bf16[4,192,128]{2,1,0:T(8,128)(2,1)} %get-tuple-element.13.select_ref, bf16[4,192,128]{2,1,0:T(8,128)(2,1)} %get-tuple-element.14.weight_ref), custom_call_target="tpu_custom_call" | custom-call | tf_op jit(solution)/shard_map/pallas_call | solution.py:410
  210.4 0.0 copy-start.8
  210.5 0.0 copy-start.13
  210.5 6.7 %fusion.10 = bf16[1,2048,768]{2,1,0:T(8,128)(2,1)} fusion(bf16[768,2048]{1,0:T(8,128)(2,1)} %bitcast.46, bf16[768,768]{1,0:T(8,128)(2,1)} %copy-done.9), kind=kOutput, calls=%fused_computation.15 | convolution fusion | flops 2417491968 | bytes 7471104 | tf_op jit(solution)/shard_map/dot_general | solution.py:33
  217.2 0.0 copy-done.8
  217.2 0.0 copy-done.13
  217.2 0.0 copy-start.6
  217.2 0.0 copy-start.11
  217.2 4.1 %fusion.11 = bf16[1,2048,768]{2,1,0:T(8,128)(2,1)} fusion(bf16[768,2048]{1,0:T(8,128)(2,1)S(1)} %bitcast.48, bf16[768,768]{1,0:T(8,128)(2,1)S(1)} %copy-done.13), kind=kOutput, calls=%fused_computation.16 | convolution fusion | flops 2417491968 | bytes 7471104 | tf_op jit(solution)/shard_map/dot_general | solution.py:34
  221.3 0.0 copy-done.6
  221.3 0.0 copy-done.11
  221.3 0.0 copy-start.2
  221.3 0.0 copy-start.1
  221.3 4.0 %fusion.12 = bf16[1,768,2048]{2,1,0:T(8,128)(2,1)} fusion(bf16[768,768]{1,0:T(8,128)(2,1)S(1)} %copy-done.11, bf16[768,2048]{1,0:T(8,128)(2,1)S(1)} %bitcast.44), kind=kOutput, calls=%fused_computation.17 | convolution fusion | flops 2417491968 | bytes 7471104 | tf_op jit(solution)/shard_map/dot_general | solution.py:32
  225.3 0.0 copy-done.2
  225.3 0.8 copy.14
  226.1 0.0 copy-done.1
  226.1 0.8 copy.15
Async XLA Ops:
  0.6 98.9 %copy-start = (bf16[1,768,2048]{2,1,0:T(8,128)(2,1)S(1)}, bf16[1,768,2048]{2,1,0:T(8,128)(2,1)}, u32[]{:S(2)}) copy-start(bf16[1,768,2048]{2,1,0:T(8,128)(2,1)} %param.13) | copy-start | bytes 9437188
  91.3 5.6 %copy-start.3 = (bf16[1,2048,768]{2,1,0:T(8,128)(2,1)S(1)}, bf16[1,2048,768]{2,1,0:T(8,128)(2,1)}, u32[]{:S(2)}) copy-start(bf16[1,2048,768]{2,1,0:T(8,128)(2,1)} %param.11) | copy-start | bytes 9437188
  91.3 5.6 %copy-start.7 = (bf16[8,4,24,2048]{3,2,1,0:T(8,128)(2,1)S(1)}, bf16[8,4,24,2048]{3,2,1,0:T(8,128)(2,1)}, u32[]{:S(2)}) copy-start(bf16[8,4,24,2048]{3,2,1,0:T(8,128)(2,1)} %get-tuple-element.11) | copy-start | bytes 9437188
  96.9 2.6 %copy-start.5 = (bf16[8,4,24,2048]{3,2,1,0:T(8,128)(2,1)S(1)}, bf16[8,4,24,2048]{3,2,1,0:T(8,128)(2,1)}, u32[]{:S(2)}) copy-start(bf16[8,4,24,2048]{3,2,1,0:T(8,128)(2,1)} %get-tuple-element.12) | copy-start | bytes 9437188
  103.0 2.7 %copy-start.9 = (bf16[768,768]{1,0:T(8,128)(2,1)}, bf16[768,768]{1,0:T(8,128)(2,1)S(1)}, u32[]{:S(2)}) copy-start(bf16[768,768]{1,0:T(8,128)(2,1)S(1)} %get-tuple-element.18) | copy-start | bytes 3538948
  103.0 2.7 %copy-start.12 = (bf16[768,768]{1,0:T(8,128)(2,1)}, bf16[768,768]{1,0:T(8,128)(2,1)S(1)}, u32[]{:S(2)}) copy-start(bf16[768,768]{1,0:T(8,128)(2,1)S(1)} %get-tuple-element.17) | copy-start | bytes 3538948
  103.0 7.2 %copy-start.10 = (bf16[768,768]{1,0:T(8,128)(2,1)}, bf16[768,768]{1,0:T(8,128)(2,1)S(1)}, u32[]{:S(2)}) copy-start(bf16[768,768]{1,0:T(8,128)(2,1)S(1)} %get-tuple-element.19) | copy-start | bytes 3538948
  103.0 3.2 %copy-start.4 = (bf16[1,2048,768]{2,1,0:T(8,128)(2,1)S(1)}, bf16[1,2048,768]{2,1,0:T(8,128)(2,1)}, u32[]{:S(2)}) copy-start(bf16[1,2048,768]{2,1,0:T(8,128)(2,1)} %param.12) | copy-start | bytes 9437188
  210.4 6.7 %copy-start.8 = (bf16[8,4,24,2048]{3,2,1,0:T(8,128)(2,1)S(1)}, bf16[8,4,24,2048]{3,2,1,0:T(8,128)(2,1)}, u32[]{:S(2)}) copy-start(bf16[8,4,24,2048]{3,2,1,0:T(8,128)(2,1)} %get-tuple-element.11) | copy-start | bytes 9437188
  210.5 6.7 %copy-start.13 = (bf16[768,768]{1,0:T(8,128)(2,1)S(1)}, bf16[768,768]{1,0:T(8,128)(2,1)}, u32[]{:S(2)}) copy-start(bf16[768,768]{1,0:T(8,128)(2,1)} %copy-done.12) | copy-start | bytes 3538948
  217.2 4.1 %copy-start.6 = (bf16[8,4,24,2048]{3,2,1,0:T(8,128)(2,1)S(1)}, bf16[8,4,24,2048]{3,2,1,0:T(8,128)(2,1)}, u32[]{:S(2)}) copy-start(bf16[8,4,24,2048]{3,2,1,0:T(8,128)(2,1)} %get-tuple-element.12) | copy-start | bytes 9437188
  217.2 4.1 %copy-start.11 = (bf16[768,768]{1,0:T(8,128)(2,1)S(1)}, bf16[768,768]{1,0:T(8,128)(2,1)}, u32[]{:S(2)}) copy-start(bf16[768,768]{1,0:T(8,128)(2,1)} %copy-done.10) | copy-start | bytes 3538948
  221.3 4.0 %copy-start.2 = (bf16[128,2048]{1,0:T(8,128)(2,1)S(1)}, bf16[128,2048]{1,0:T(8,128)(2,1)}, u32[]{:S(2)}) copy-start(bf16[128,2048]{1,0:T(8,128)(2,1)} %get-tuple-element.25) | copy-start | bytes 1572868
  221.3 4.8 %copy-start.1 = (bf16[128,2048]{1,0:T(8,128)(2,1)S(1)}, bf16[128,2048]{1,0:T(8,128)(2,1)}, u32[]{:S(2)}) copy-start(bf16[128,2048]{1,0:T(8,128)(2,1)} %get-tuple-element.26) | copy-start | bytes 1572868
